TPU v7x, 32 devices: a whole 2x2x4 slice. The times are simulated.
32 devices in a mesh: tp: 4 (over y, x), rep: 8 (over z, core).
Axes of the slice: x: 2, y: 2, z: 4, core: 2. Of those that a mesh axis runs over, the one named last changes fastest.
Arguments:
- queries: bfloat16 [128, 4096], P('rep', 'tp'), may hold values from -6 to 6
- new_keys: bfloat16 [128, 2048], P('rep', 'tp'), may hold values from -6 to 6
- new_values: bfloat16 [128, 2048], P('rep', 'tp'), may hold values from -6 to 6
- stored_keys: bfloat16 [128, 16, 128, 128], P('rep', 'tp'), may hold values from -6 to 6
- stored_values: bfloat16 [128, 16, 128, 128], P('rep', 'tp'), may hold values from -6 to 6
- lengths: int32 [128], P('rep'), may hold values from 1 to 128
- out_proj: bfloat16 [4096, 4608], P('tp', 'rep'), may hold values from -0.09375 to 0.09375
- residual: bfloat16 [128, 4608], P(None, 'rep'), may hold values from -4.5 to 4.5
- norm_gain: float32 [4608], replicated, may hold values from 0.1 to 1.9
- embedding: bfloat16 [256000, 4608], P(('tp', 'rep')), may hold values from -1.25 to 1.25
- targets: int32 [128], replicated, may hold values from 0 to 255999
- old_sums: float32 [128], P('rep'), may hold values from -3 to 0
- rewards: float32 [128], P('rep'), may hold values from -6 to 6
- group_ids: int32 [128], P('rep'), may hold values from 0 to 15, as said below
Outputs:
- logprob_sum: float32 [128], P('rep')
- advantage: float32 [128], P('rep')
Inputs may be any that keep to these rules, and one draw needn't show every extreme that they name: `group_ids`: each id names exactly 8 continuations.
All inputs are finite; a program needn't handle non-finite values.
Results may differ from a plain program's by a relative error of at most 0.001.
Values may be sent and summed in bfloat16 or wider, within the bound.
A program may use at most 128 MiB of HBM per device.

v0:
```python
import jax
import jax.numpy as jnp
from jax import lax
from jax.sharding import PartitionSpec as P

GROUP = 8


def attention(queries, new_keys, new_values, stored_keys, stored_values, lengths):
    samp, heads_kv, span, depth = stored_keys.shape
    sample_ratio = queries.shape[1] // (heads_kv * depth)
    query_vector = queries.reshape(samp, heads_kv, sample_ratio, depth)
    scores = (
        jnp.einsum("sgqd,sgpd->sgqp", query_vector, stored_keys, preferred_element_type=jnp.float32)
        / 12.0
    )
    scores = 50.0 * jnp.tanh(scores / 50.0)
    valid = lax.broadcasted_iota(jnp.int32, (samp, 1, 1, span), 3) < lengths[:, None, None, None]
    expo = jnp.where(valid, jnp.exp(scores), 0.0)
    own_logit = (
        jnp.einsum(
            "sgqd,sgd->sgq",
            query_vector,
            new_keys.reshape(samp, heads_kv, depth),
            preferred_element_type=jnp.float32,
        )
        / 12.0
    )
    own_logit = 50.0 * jnp.tanh(own_logit / 50.0)
    own_exp = jnp.exp(own_logit)
    total = jnp.sum(expo, -1) + own_exp
    probs = (expo / total[..., None]).astype(jnp.bfloat16)
    own_probability = (own_exp / total).astype(jnp.bfloat16)
    attended_output = jnp.einsum(
        "sgqp,sgpd->sgqd", probs, stored_values, preferred_element_type=jnp.float32
    )
    attended_output = attended_output + own_probability.astype(jnp.float32)[
        ..., None
    ] * new_values.reshape(samp, heads_kv, 1, depth).astype(jnp.float32)
    return attended_output.reshape(samp, sample_ratio * heads_kv * depth).astype(jnp.bfloat16)


def per_device(
    queries,
    new_keys,
    new_values,
    stored_keys,
    stored_values,
    lengths,
    out_proj,
    residual,
    norm_gain,
    embedding,
    targets,
    old_sums,
    rewards,
    group_ids,
):
    samp = queries.shape[0]
    reps = lax.axis_size("rep")
    rep_index = lax.axis_index("rep")
    tp_index = lax.axis_index("tp")
    groups = samp * reps // GROUP
    member = group_ids[:, None] == lax.broadcasted_iota(jnp.int32, (1, groups), 1)
    reward_part = jnp.sum(jnp.where(member, rewards[:, None], 0.0), 0)
    group_total = lax.psum(reward_part, "rep")
    mine = jnp.sum(jnp.where(member, group_total[None, :], 0.0), 1)
    advantage = rewards - (mine - rewards) / (GROUP - 1.0)
    context = attention(queries, new_keys, new_values, stored_keys, stored_values, lengths)
    partial_value = jnp.dot(
        lax.all_gather(context, "rep", axis=0, tiled=True),
        out_proj,
        preferred_element_type=jnp.float32,
    )
    vocab_rows = embedding.shape[0]
    contract = (((1,), (1,)), ((), ()))
    heads = lax.psum(partial_value, "tp")
    stream = residual.astype(jnp.float32) + heads
    full = lax.all_gather(stream, "rep", axis=1, tiled=True)
    scale = lax.rsqrt(jnp.mean(full * full, axis=1, keepdims=True) + 1e-06)
    normed = (full * scale * norm_gain[None, :]).astype(jnp.bfloat16)
    logits = lax.dot_general(normed, embedding, contract, preferred_element_type=jnp.float32)
    capped = 30.0 * jnp.tanh(logits / 30.0)
    offset = (tp_index * reps + rep_index) * vocab_rows
    entry_ids = offset + lax.broadcasted_iota(jnp.int32, (1, vocab_rows), 1)
    picked_part = jnp.sum(jnp.where(entry_ids == targets[:, None], capped, 0.0), 1)
    total, picked = lax.psum((jnp.sum(jnp.exp(capped), 1), picked_part), ("tp", "rep"))
    logprob = picked - jnp.log(total)
    own_rows = lax.dynamic_slice_in_dim(logprob, rep_index * samp, samp)
    logprob_sum = old_sums + own_rows
    return (logprob_sum, advantage)


def solution(mesh):
    in_specs = (
        P("rep", "tp"),
        P("rep", "tp"),
        P("rep", "tp"),
        P("rep", "tp", None, None),
        P("rep", "tp", None, None),
        P("rep"),
        P("tp", "rep"),
        P(None, "rep"),
        P(),
        P(("tp", "rep"), None),
        P(),
        P("rep"),
        P("rep"),
        P("rep"),
    )
    out_specs = (P("rep"), P("rep"))
    return jax.shard_map(
        per_device, mesh=mesh, in_specs=in_specs, out_specs=out_specs, check_vma=False
    )
```

profile of v0, /device:TPU:0, one launch (start us, length us, event | category | flops | bytes accessed | tf_op | source)
XLA Modules:
  0.0 191.0 jit_solution(11185303319291343823)
XLA Ops:
  7.2 0.0 copy-start
  7.2 0.0 copy-start.4
  7.2 0.0 all-reduce.3.cloned.1.call-start
  7.2 0.9 reshape.60
  8.2 0.7 iota_compare_fusion.1
  8.9 0.0 copy-done
  8.9 1.3 fusion.15
  10.2 0.0 copy-start.2
  10.2 0.1 copy.18
  10.3 0.8 reshape.66
  11.1 0.2 fusion.16
  11.3 0.1 copy.22
  11.4 0.1 copy.19
  11.6 0.1 copy.20
  11.7 0.0 copy-done.4
  11.7 0.6 reshape.62
  12.3 0.0 copy-start.3
  12.3 2.9 %fusion.8 = bf16[16,4,2,128]{3,2,1,0:T(2,128)(2,1)} fusion(bf16[16,4,128,128]{3,2,1,0:T(8,128)(2,1)} %param.18, f32[16,4,2,128]{3,2,1,0:T(2,128)S(1)} %get-tuple-element.9, f32[16,4,128]{2,1,0:T(4,128)} %reshape.62, f32[16,4,2]{2,1,0:T(4,128)S(1)} %copy.20, f32[16,4,2]{2,1,0:T(4,128)S(1)} %copy.19), kind=kOutput, calls=%fused_computation.15 | convolution fusion | flops 4276224 | bytes 2229248 | tf_op jit(solution)/shard_map/sgqp,sgpd->sgqd/dot_general | solution.py:34
  15.2 0.0 copy-start.7
  15.2 0.0 copy-start.8
  15.2 0.8 convert_element_type.39
  16.1 15.9 %all_gather.6 = bf16[128,1024]{1,0:T(8,128)(2,1)S(1)} all-gather(bf16[16,1024]{1,0:T(8,128)(2,1)S(1)} %convert_element_type.39), channel_id=1, replica_groups=mesh['tp'=4,'rep'=8] {'rep'}, dimensions={0}, use_global_device_ids=true | all-gather | bytes 294912 | tf_op jit(solution)/shard_map/all_gather | solution.py:71
  32.0 0.0 copy-done.2
  32.0 0.0 copy-start.6
  32.0 0.0 copy-start.9
  32.0 1.2 fusion.17
  33.2 0.0 all-reduce.3.cloned.1.call-update
  33.2 0.0 all-gather.2.cloned.1.call-start
  33.2 44.5 %all-reduce.3.cloned.1.call-done = f32[128,576]{0,1:T(8,128)} async-done(((f32[128,576]{0,1:T(8,128)}), f32[128,576]{0,1:T(8,128)}) %all-reduce.3.cloned.1.call-update) | async-done | bytes 294928 | tf_op jit(solution)/shard_map/psum | solution.py:77
  77.7 0.0 copy-done.3
  77.7 1.7 convert_add_fusion
  79.4 0.0 all-gather.2.cloned.1.call-update
  79.5 0.0 copy-done.7
  79.5 0.0 copy-done.8
  79.5 0.1 select_reduce_fusion.2
  79.6 16.4 %psum.31 = f32[16]{0:T(128)S(1)} all-reduce(f32[16]{0:T(128)S(1)} %select_reduce_fusion.2), channel_id=1, replica_groups=mesh['tp'=4,'rep'=8] {'rep'}, use_global_device_ids=true, to_apply=%region_8.9 | all-reduce | flops 16 | bytes 128 | tf_op jit(solution)/shard_map/psum | solution.py:66
  96.0 0.2 select_reduce_fusion.1
  96.2 0.5 multiply_subtract_fusion
  96.7 14.5 %all-gather.2.cloned.1.call-done = f32[128,4608]{0,1:T(8,128)} async-done(((f32[128,576]{0,1:T(8,128)}), f32[128,4608]{0,1:T(8,128)}) %all-gather.2.cloned.1.call-update) | async-done | bytes 2359312 | tf_op jit(solution)/shard_map/all_gather | solution.py:79
  111.2 2.4 %multiply_reduce_fusion = f32[128]{0:T(128)S(1)} fusion(f32[128,4608]{0,1:T(8,128)} %all-gather.2.cloned.1.call-done), kind=kLoop, calls=%fused_computation.6 | loop fusion | flops 1179520 | bytes 2359808 | tf_op jit(solution)/shard_map/reduce_sum | solution.py:80
  113.6 0.0 copy-done.6
  113.6 0.0 copy-done.9
  113.6 0.0 copy-done.1
  113.7 0.0 copy-start.5
  113.7 30.2 %exponential_reduce_fusion = (f32[128]{0:T(128)S(1)}, f32[128]{0:T(128)S(1)}) fusion(s32[128]{0:T(128)S(1)} %copy-done.9, s32[8000]{0:T(1024)S(1)} %iota_add_fusion, bf16[8000,4608]{1,0:T(8,128)(2,1)} %param.23, f32[128,4608]{0,1:T(8,128)S(1)} %copy-done.1, f32[4608]{0:T(1024)S(1)} %copy-done.6, f32[128]{0:T(128)S(1)} %add_rsqrt_fusion), kind=kOutput, calls=%fused_computation.3 | convolution fusion | flops 9445097472 | bytes 76139776 | tf_op jit(solution)/shard_map/dot_general | solution.py:82
  143.8 39.7 %all-reduce = (f32[128]{0:T(128)S(1)}, f32[128]{0:T(128)S(1)}) all-reduce(f32[128]{0:T(128)S(1)} %get-tuple-element.3, f32[128]{0:T(128)S(1)} %get-tuple-element.2), channel_id=1, replica_groups=mesh['tp'=4,'rep'=8] {'tp','rep'}, use_global_device_ids=true, to_apply=%region_4.5 | all-reduce | flops 256 | bytes 2048 | tf_op jit(solution)/shard_map/psum | solution.py:87
  183.6 0.0 copy-done.5
  183.6 0.6 dynamic-slice_add_fusion
  (5 shorter events, 0.0 us)
Async XLA Ops:
  7.2 1.7 copy-start
  7.2 4.5 %copy-start.4 = (bf16[16,512]{1,0:T(8,128)(2,1)S(1)}, bf16[16,512]{1,0:T(8,128)(2,1)}, u32[]{:S(2)}) copy-start(bf16[16,512]{1,0:T(8,128)(2,1)} %param.16) | copy-start | bytes 49156
  7.2 70.5 %all-reduce.3.cloned.1.call-start = ((), (), s32[]{:S(2)}) async-start(), calls=%async_computation | async-start | bytes 589824 | tf_op jit(solution)/shard_map/psum | solution.py:77
  10.2 21.8 %copy-start.2 = (bf16[1024,576]{0,1:T(8,128)(2,1)S(1)}, bf16[1024,576]{0,1:T(8,128)(2,1)}, u32[]{:S(2)}) copy-start(bf16[1024,576]{0,1:T(8,128)(2,1)} %param.20) | copy-start | bytes 3538948
  12.3 65.4 %copy-start.3 = (bf16[128,576]{0,1:T(8,128)(2,1)S(1)}, bf16[128,576]{0,1:T(8,128)(2,1)}, u32[]{:S(2)}) copy-start(bf16[128,576]{0,1:T(8,128)(2,1)} %param.21) | copy-start | bytes 442372
  15.2 64.2 %copy-start.7 = (s32[16]{0:T(128)S(1)}, s32[16]{0:T(128)}, u32[]{:S(2)}) copy-start(s32[16]{0:T(128)} %param.27) | copy-start | bytes 196
  15.2 64.2 %copy-start.8 = (f32[16]{0:T(128)S(1)}, f32[16]{0:T(128)}, u32[]{:S(2)}) copy-start(f32[16]{0:T(128)} %param.26) | copy-start | bytes 196
  32.0 81.7 %copy-start.6 = (f32[4608]{0:T(1024)S(1)}, f32[4608]{0:T(1024)}, u32[]{:S(2)}) copy-start(f32[4608]{0:T(1024)} %param.22) | copy-start | bytes 55300
  32.0 81.7 %copy-start.9 = (s32[128]{0:T(128)S(1)}, s32[128]{0:T(128)}, u32[]{:S(2)}) copy-start(s32[128]{0:T(128)} %param.24) | copy-start | bytes 1540
  33.2 78.0 %all-gather.2.cloned.1.call-start = ((), (), s32[]{:S(2)}) async-start(), calls=%async_computation.1 | async-start | bytes 2654208 | tf_op jit(solution)/shard_map/all_gather | solution.py:79
  111.2 2.5 %copy-start.1 = (f32[128,4608]{0,1:T(8,128)S(1)}, f32[128,4608]{0,1:T(8,128)}, u32[]{:S(2)}) copy-start(f32[128,4608]{0,1:T(8,128)} %all-gather.2.cloned.1.call-done) | copy-start | bytes 7077892
  113.7 69.9 %copy-start.5 = (f32[16]{0:T(128)S(1)}, f32[16]{0:T(128)}, u32[]{:S(2)}) copy-start(f32[16]{0:T(128)} %param.25) | copy-start | bytes 196
Sparse Core Ops, SparseCore 0:
  33.3 44.3 all-reduce.2
  79.6 31.5 all-gather.1
where the time goes:
time: 191 us
  blocking collectives  72.1 us (38%)
  waiting for transfers between devices  59 us (31%)
  matrix products  35.8 us (19%)
  between operations  14.1 us (7%)
  other arithmetic  6.3 us (3%)
  local copies, waits for them, and re-layouts  3.63 us (2%)
    psum x1, waiting for transfers between devices, per_device(): heads = lax.psum(partial_value, 'tp')  44.5 us
    psum x1, blocking collectives, per_device(): lax.psum((jnp.sum(jnp.exp(capped), 1), picked_part), ('tp', 'rep'))  39.7 us
    dot_general x1, matrix products, per_device(): lax.dot_general(normed, embedding, contract, preferred_element_type=jnp.f...  30.2 us
    psum x1, blocking collectives, per_device(): group_total = lax.psum(reward_part, 'rep')  16.4 us
    all_gather x1, blocking collectives, per_device(): lax.all_gather(context, 'rep', axis=0, tiled=True)  15.9 us
    all_gather x1, waiting for transfers between devices, per_device(): full = lax.all_gather(stream, 'rep', axis=1, tiled=True)  14.5 us
  transfers between devices with their start and end apart: 2, of which 2 were waited for; matrix products, arithmetic and copies ran while one was open for 0% of the time, Pallas kernels for 0%

commit v1 on v0

--- a/solution.py
+++ b/solution.py
@@ -1,7 +1,16 @@
+import functools
+
 import jax
 import jax.numpy as jnp
 from jax import lax
+from jax.experimental import pallas as pl
+from jax.experimental.pallas import tpu as pltpu
 from jax.sharding import PartitionSpec as P
+
+MESH = pl.DeviceIdType.MESH
+ROWS_PER_BLOCK = 512
+SLOTS = 10
+VMEM_BYTES = 66 * 1000 * 1000
 
 GROUP = 8
 
@@ -91,6 +100,463 @@
     return (logprob_sum, advantage)
 
 
+def as_column(row, count):
+    eye = lax.broadcasted_iota(jnp.int32, (count, count), 0) == lax.broadcasted_iota(
+        jnp.int32, (count, count), 1
+    )
+    return jnp.sum(jnp.where(eye, row, 0.0), 1, keepdims=True)
+
+
+def as_row(column, count):
+    eye = lax.broadcasted_iota(jnp.int32, (count, count), 0) == lax.broadcasted_iota(
+        jnp.int32, (count, count), 1
+    )
+    return jnp.sum(jnp.where(eye, column, 0.0), 0, keepdims=True)
+
+
+def step_kernel(
+    tps,
+    reps,
+    lengths,
+    queries,
+    new_keys,
+    new_values,
+    residual,
+    gain,
+    targets,
+    old_sums,
+    rewards,
+    group_ids,
+    keys_hbm,
+    values_hbm,
+    proj_hbm,
+    table_hbm,
+    logprob_out,
+    advantage_out,
+    keys,
+    values,
+    proj,
+    table,
+    q_rows,
+    nk_rows,
+    nv_rows,
+    ctx_rows,
+    context,
+    partial,
+    reduced,
+    blocks,
+    normed,
+    reward_rows,
+    final_tp,
+    final_rep,
+    local_sem,
+    table_sem,
+    send_sem,
+    ctx_sem,
+    red_sem,
+    block_sem,
+    reward_sem,
+    ftp_sem,
+    frep_sem,
+):
+    t = lax.axis_index("tp")
+    r = lax.axis_index("rep")
+    samp, heads_kv, span, depth = keys_hbm.shape
+    heads = queries.shape[1] // depth
+    ratio = heads // heads_kv
+    total_samp = samp * reps
+    cols = residual.shape[1]
+    padded = blocks.shape[2]
+    share = total_samp // tps
+    vocab_rows, width = table_hbm.shape
+    full = vocab_rows // ROWS_PER_BLOCK
+    tail = vocab_rows - full * ROWS_PER_BLOCK
+    zs = reps // 2
+    core = lax.rem(r, 2)
+    partner = r + 1 - 2 * core
+    sent = []
+
+    def table_copy(index, slot):
+        return pltpu.make_async_copy(
+            table_hbm.at[pl.ds(pl.multiple_of(index * ROWS_PER_BLOCK, ROWS_PER_BLOCK), ROWS_PER_BLOCK)],
+            table.at[slot],
+            table_sem.at[slot],
+        )
+
+    def tail_copy():
+        slot = full % SLOTS
+        return pltpu.make_async_copy(
+            table_hbm.at[pl.ds(full * ROWS_PER_BLOCK, tail)],
+            table.at[slot, pl.ds(0, tail)],
+            table_sem.at[slot],
+        )
+
+    key_copies = [pltpu.make_async_copy(keys_hbm, keys, local_sem.at[0])]
+    value_copies = [pltpu.make_async_copy(values_hbm, values, local_sem.at[1])]
+    proj_copy = pltpu.make_async_copy(proj_hbm, proj, local_sem.at[2])
+    for copy in key_copies + value_copies + [proj_copy]:
+        copy.start()
+    for index in range(SLOTS):
+        table_copy(index, index).start()
+
+    barrier = pltpu.get_barrier_semaphore()
+    for k in range(1, tps):
+        pl.semaphore_signal(
+            barrier, inc=1, device_id=(lax.rem(t + k, tps), r), device_id_type=MESH
+        )
+    for k in range(1, reps):
+        pl.semaphore_signal(
+            barrier, inc=1, device_id=(t, lax.rem(r + k, reps)), device_id_type=MESH
+        )
+
+    def send(src, dst, recv, device):
+        copy = pltpu.make_async_remote_copy(
+            src_ref=src,
+            dst_ref=dst,
+            send_sem=send_sem.at[len(sent)],
+            recv_sem=recv,
+            device_id=device,
+            device_id_type=MESH,
+        )
+        copy.start()
+        sent.append(copy)
+
+    def received(ref, recv):
+        pltpu.make_async_remote_copy(
+            src_ref=ref,
+            dst_ref=ref,
+            send_sem=send_sem.at[0],
+            recv_sem=recv,
+            device_id=(t, partner),
+            device_id_type=MESH,
+        ).wait_recv()
+
+    reward_rows[r] = jnp.zeros(reward_rows.shape[1:], jnp.float32)
+    reward_rows[r, 0:1, 0:samp] = rewards[...]
+    reward_rows[r, 1:2, 0:samp] = group_ids[...].astype(jnp.float32)
+
+    for h in range(heads):
+        g = h // ratio
+        q_rows[:, h, :] = queries[:, h * depth : (h + 1) * depth].astype(jnp.float32)
+        nk_rows[:, h, :] = new_keys[:, g * depth : (g + 1) * depth].astype(jnp.float32)
+        nv_rows[:, h, :] = new_values[:, g * depth : (g + 1) * depth].astype(jnp.float32)
+
+    head_group = lax.broadcasted_iota(jnp.int32, (heads, span), 0) // ratio
+    position = lax.broadcasted_iota(jnp.int32, (heads, span), 1)
+    for copy in key_copies:
+        copy.wait()
+    probs = []
+    own_probs = []
+    for s in range(samp):
+        query = q_rows[s]
+        wide = lax.dot_general(
+            query.astype(jnp.bfloat16),
+            keys[s].reshape(heads_kv * span, depth),
+            (((1,), (1,)), ((), ())),
+            preferred_element_type=jnp.float32,
+        )
+        scores = wide[:, 0:span]
+        for g in range(1, heads_kv):
+            scores = jnp.where(head_group == g, wide[:, g * span : (g + 1) * span], scores)
+        scores = 50.0 * jnp.tanh(scores / 12.0 / 50.0)
+        expo = jnp.where(position < lengths[s], jnp.exp(scores), 0.0)
+        own = jnp.sum(query * nk_rows[s], 1, keepdims=True) / 12.0
+        own_exp = jnp.exp(50.0 * jnp.tanh(own / 50.0))
+        total = jnp.sum(expo, 1, keepdims=True) + own_exp
+        probs.append((expo / total).astype(jnp.bfloat16).astype(jnp.float32))
+        own_probs.append((own_exp / total).astype(jnp.bfloat16).astype(jnp.float32))
+    for copy in value_copies:
+        copy.wait()
+    for s in range(samp):
+        spread = jnp.concatenate(
+            [jnp.where(head_group == g, probs[s], 0.0) for g in range(heads_kv)], axis=1
+        )
+        attended = jnp.dot(
+            spread.astype(jnp.bfloat16),
+            values[s].reshape(heads_kv * span, depth),
+            preferred_element_type=jnp.float32,
+        )
+        ctx_rows[s] = attended + own_probs[s] * nv_rows[s]
+    own_ctx = context.at[pl.ds(pl.multiple_of(r * samp, samp), samp)]
+    for h in range(heads):
+        own_ctx[:, h * depth : (h + 1) * depth] = ctx_rows[:, h, :].astype(jnp.bfloat16)
+
+    pl.semaphore_wait(barrier, tps + reps - 2)
+
+    def ctx_slot(q):
+        return context.at[pl.ds(pl.multiple_of(q * samp, samp), samp)]
+
+    for k in range(1, zs):
+        send(ctx_slot(r), ctx_slot(r), ctx_sem.at[r], (t, lax.rem(r + 2 * k, reps)))
+    send(ctx_slot(r), ctx_slot(r), ctx_sem.at[r], (t, partner))
+    for k in range(1, reps):
+        send(reward_rows.at[r], reward_rows.at[r], reward_sem.at[r], (t, lax.rem(r + k, reps)))
+    for k in range(1, zs):
+        q = lax.rem(r + 2 * k, reps)
+        received(ctx_slot(q), ctx_sem.at[q])
+        send(ctx_slot(q), ctx_slot(q), ctx_sem.at[q], (t, partner))
+    for k in range(zs):
+        q = lax.rem(partner + 2 * k, reps)
+        received(ctx_slot(q), ctx_sem.at[q])
+
+    proj_copy.wait()
+    product = jnp.dot(context[...], proj[...], preferred_element_type=jnp.float32)
+    for k in range(tps):
+        partial[k] = product[k * share : (k + 1) * share]
+    for k in range(1, tps):
+        u = lax.rem(t + k, tps)
+        send(partial.at[u], reduced.at[t], red_sem.at[t], (u, r))
+    reduced[t] = partial[t]
+    own_gain = gain[:, 0:cols]
+    for q in range(1, reps):
+        own_gain = jnp.where(r == q, gain[:, q * cols : (q + 1) * cols], own_gain)
+    rest = residual[pl.ds(pl.multiple_of(t * share, share), share)].astype(jnp.float32)
+    for k in range(1, tps):
+        u = lax.rem(t + k, tps)
+        received(reduced.at[u], red_sem.at[u])
+    stream = reduced[0]
+    for k in range(1, tps):
+        stream = stream + reduced[k]
+    stream = stream + rest
+    square = jnp.sum(stream * stream, 1, keepdims=True)
+    high = square.astype(jnp.bfloat16).astype(jnp.float32)
+    mid = (square - high).astype(jnp.bfloat16).astype(jnp.float32)
+    low = square - high - mid
+    lane = lax.broadcasted_iota(jnp.int32, (share, padded - cols), 1)
+    extra = jnp.where(lane == 0, high, jnp.where(lane == 1, mid, jnp.where(lane == 2, low, 0.0)))
+    mine = blocks.at[r, pl.ds(pl.multiple_of(t * share, share), share)]
+    mine[:, 0:cols] = (stream * own_gain).astype(jnp.bfloat16)
+    mine[:, cols:padded] = extra.astype(jnp.bfloat16)
+
+    def block(u, q):
+        return blocks.at[q, pl.ds(pl.multiple_of(u * share, share), share)]
+
+    def arrived(u, q):
+        return block_sem.at[u * reps + q]
+
+    for k in range(1, zs):
+        send(block(t, r), block(t, r), arrived(t, r), (t, lax.rem(r + 2 * k, reps)))
+    for step in range(zs):
+        q = lax.rem(r + 2 * step, reps)
+        if step:
+            received(block(t, q), arrived(t, q))
+        for k in range(1, tps):
+            send(block(t, q), block(t, q), arrived(t, q), (lax.rem(t + k, tps), r))
+        send(block(t, q), block(t, q), arrived(t, q), (t, partner))
+    for step in range(zs):
+        q = lax.rem(r + 2 * step, reps)
+        for k in range(1, tps):
+            u = lax.rem(t + k, tps)
+            received(block(u, q), arrived(u, q))
+            send(block(u, q), block(u, q), arrived(u, q), (t, partner))
+    for step in range(zs):
+        q = lax.rem(partner + 2 * step, reps)
+        for k in range(tps):
+            u = lax.rem(t + k, tps)
+            received(block(u, q), arrived(u, q))
+
+    squares = jnp.zeros((total_samp, 1), jnp.float32)
+    for z in range(zs):
+        left = blocks[2 * z].astype(jnp.float32)
+        right = blocks[2 * z + 1].astype(jnp.float32)
+        pair = jnp.concatenate([left[:, 0:cols], right[:, 0:cols]], axis=1)
+        normed[:, 2 * z * cols : 2 * (z + 1) * cols] = pair.astype(jnp.bfloat16)
+        squares = squares + jnp.sum(left[:, cols:padded], 1, keepdims=True)
+        squares = squares + jnp.sum(right[:, cols:padded], 1, keepdims=True)
+    scale = lax.rsqrt(squares / width + 1e-06)
+    wanted = as_column(targets[...].astype(jnp.float32), total_samp).astype(jnp.int32)
+    wanted = wanted - (t * reps + r) * vocab_rows
+
+    def score(rows, first, carry):
+        total, picked = carry
+        logits = lax.dot_general(
+            normed[...], rows, (((1,), (1,)), ((), ())), preferred_element_type=jnp.float32
+        )
+        capped = 30.0 * jnp.tanh(logits * scale / 30.0)
+        entry = lax.broadcasted_iota(jnp.int32, capped.shape, 1) + first
+        total = total + jnp.sum(jnp.exp(capped), 1, keepdims=True)
+        picked = picked + jnp.sum(jnp.where(entry == wanted, capped, 0.0), 1, keepdims=True)
+        return total, picked
+
+    def visit(index, carry):
+        slot = lax.rem(index, SLOTS)
+        table_copy(index, slot).wait()
+        carry = score(table[slot], index * ROWS_PER_BLOCK, carry)
+
+        @pl.when(index + SLOTS < full)
+        def _():
+            table_copy(index + SLOTS, slot).start()
+
+        if tail:
+
+            @pl.when(index + SLOTS == full)
+            def _():
+                tail_copy().start()
+
+        return carry
+
+    zero = jnp.zeros((total_samp, 1), jnp.float32)
+    carry = lax.fori_loop(0, full, visit, (zero, zero))
+    if tail:
+        tail_copy().wait()
+        carry = score(table[full % SLOTS, 0:tail], full * ROWS_PER_BLOCK, carry)
+
+    final_tp[t] = jnp.zeros(final_tp.shape[1:], jnp.float32)
+    final_tp[t, 0:1] = as_row(carry[0], total_samp)
+    final_tp[t, 1:2] = as_row(carry[1], total_samp)
+    for k in range(1, tps):
+        send(final_tp.at[t], final_tp.at[t], ftp_sem.at[t], (lax.rem(t + k, tps), r))
+
+    for k in range(1, reps):
+        q = lax.rem(r + k, reps)
+        received(reward_rows.at[q], reward_sem.at[q])
+    own_ids = as_column(group_ids[...].astype(jnp.float32), samp)
+    group_sum = jnp.zeros((samp, 1), jnp.float32)
+    for q in range(reps):
+        same = own_ids == reward_rows[q, 1:2, 0:samp]
+        group_sum = group_sum + jnp.sum(
+            jnp.where(same, reward_rows[q, 0:1, 0:samp], 0.0), 1, keepdims=True
+        )
+    group_sum = as_row(group_sum, samp)
+    advantage_out[...] = rewards[...] - (group_sum - rewards[...]) / (GROUP - 1.0)
+
+    for k in range(1, tps):
+        u = lax.rem(t + k, tps)
+        received(final_tp.at[u], ftp_sem.at[u])
+    column = final_tp[0]
+    for k in range(1, tps):
+        column = column + final_tp[k]
+    final_rep[r] = column
+    for k in range(1, reps):
+        send(final_rep.at[r], final_rep.at[r], frep_sem.at[r], (t, lax.rem(r + k, reps)))
+    for k in range(1, reps):
+        q = lax.rem(r + k, reps)
+        received(final_rep.at[q], frep_sem.at[q])
+    whole = final_rep[0]
+    for k in range(1, reps):
+        whole = whole + final_rep[k]
+    logprob = whole[1:2] - jnp.log(whole[0:1])
+    chosen = lax.broadcasted_iota(jnp.int32, (samp, total_samp), 1) == (
+        lax.broadcasted_iota(jnp.int32, (samp, total_samp), 0) + r * samp
+    )
+    own_rows = jnp.sum(jnp.where(chosen, logprob, 0.0), 1, keepdims=True)
+    logprob_out[...] = old_sums[...] + as_row(own_rows, samp)
+    for copy in sent:
+        copy.wait_send()
+
+
+def one_kernel(
+    queries,
+    new_keys,
+    new_values,
+    stored_keys,
+    stored_values,
+    lengths,
+    out_proj,
+    residual,
+    norm_gain,
+    embedding,
+    targets,
+    old_sums,
+    rewards,
+    group_ids,
+):
+    tps, reps = lax.axis_size("tp"), lax.axis_size("rep")
+    samp, heads_kv, span, depth = stored_keys.shape
+    heads = queries.shape[1] // depth
+    total_samp = samp * reps
+    cols = out_proj.shape[1]
+    padded = (cols + 3 + 127) // 128 * 128
+    share = total_samp // tps
+    zs = reps // 2
+    sends = (
+        (zs - 1) + zs + (reps - 1) + (tps - 1) + (zs - 1) + zs * (tps - 1) + zs * tps
+        + (tps - 1) + (reps - 1)
+    )
+    vmem = pl.BlockSpec(memory_space=pltpu.VMEM)
+    smem = pl.BlockSpec(memory_space=pltpu.SMEM)
+    hbm = pl.BlockSpec(memory_space=pltpu.HBM)
+    dma = pltpu.SemaphoreType.DMA
+    logprob, advantage = pl.pallas_call(
+        functools.partial(step_kernel, tps, reps),
+        out_shape=[jax.ShapeDtypeStruct((1, samp), jnp.float32)] * 2,
+        in_specs=[smem] + [vmem] * 9 + [hbm] * 4,
+        out_specs=[vmem, vmem],
+        scratch_shapes=[
+            pltpu.VMEM(stored_keys.shape, stored_keys.dtype),
+            pltpu.VMEM(stored_values.shape, stored_values.dtype),
+            pltpu.VMEM(out_proj.shape, out_proj.dtype),
+            pltpu.VMEM((SLOTS, ROWS_PER_BLOCK, embedding.shape[1]), embedding.dtype),
+            pltpu.VMEM((samp, heads, depth), jnp.float32),
+            pltpu.VMEM((samp, heads, depth), jnp.float32),
+            pltpu.VMEM((samp, heads, depth), jnp.float32),
+            pltpu.VMEM((samp, heads, depth), jnp.float32),
+            pltpu.VMEM((total_samp, heads * depth), jnp.bfloat16),
+            pltpu.VMEM((tps, share, cols), jnp.float32),
+            pltpu.VMEM((tps, share, cols), jnp.float32),
+            pltpu.VMEM((reps, total_samp, padded), jnp.bfloat16),
+            pltpu.VMEM((total_samp, embedding.shape[1]), jnp.bfloat16),
+            pltpu.VMEM((reps, 8, 128), jnp.float32),
+            pltpu.VMEM((tps, 8, total_samp), jnp.float32),
+            pltpu.VMEM((reps, 8, total_samp), jnp.float32),
+            dma((3,)),
+            dma((SLOTS,)),
+            dma((sends,)),
+            dma((reps,)),
+            dma((tps,)),
+            dma((tps * reps,)),
+            dma((reps,)),
+            dma((tps,)),
+            dma((reps,)),
+        ],
+        compiler_params=pltpu.CompilerParams(
+            collective_id=0, has_side_effects=True, vmem_limit_bytes=VMEM_BYTES
+        ),
+        name="decode_step",
+    )(
+        lengths,
+        queries,
+        new_keys,
+        new_values,
+        residual,
+        norm_gain.reshape(1, -1),
+        targets.reshape(1, -1),
+        old_sums.reshape(1, -1),
+        rewards.reshape(1, -1),
+        group_ids.reshape(1, -1),
+        stored_keys,
+        stored_values,
+        out_proj,
+        embedding,
+    )
+    return logprob.reshape(-1), advantage.reshape(-1)
+
+
+def fits_one_kernel(tps, reps, stored_keys, out_proj, residual, embedding):
+    samp, heads_kv, span, depth = stored_keys.shape
+    total_samp = samp * reps
+    return (
+        span == 128
+        and depth == 128
+        and samp % 16 == 0
+        and samp <= 128
+        and reps % 2 == 0
+        and total_samp == 128
+        and total_samp % (16 * tps) == 0
+        and 2 * out_proj.shape[1] % 128 == 0
+        and embedding.shape[0] >= SLOTS * ROWS_PER_BLOCK
+        and embedding.shape[0] % 16 == 0
+        and embedding.shape[1] == reps * out_proj.shape[1]
+    )
+
+
+def per_device_best(*args):
+    tps, reps = lax.axis_size("tp"), lax.axis_size("rep")
+    if fits_one_kernel(tps, reps, args[3], args[6], args[7], args[9]):
+        return one_kernel(*args)
+    return per_device(*args)
+
+
 def solution(mesh):
     in_specs = (
         P("rep", "tp"),
@@ -110,5 +576,5 @@
     )
     out_specs = (P("rep"), P("rep"))
     return jax.shard_map(
-        per_device, mesh=mesh, in_specs=in_specs, out_specs=out_specs, check_vma=False
-    )
+        per_device_best, mesh=mesh, in_specs=in_specs, out_specs=out_specs, check_vma=False
+    )

time: 191 us -> 87.3 us (0.46)
  Pallas kernels: 0 us -> 78.6 us
  blocking collectives: 72.1 us -> 0 us
  waiting for transfers between devices: 59 us -> 0 us
  matrix products: 35.8 us -> 0 us
  between operations: 14.1 us -> 0.64 us
  other arithmetic: 6.3 us -> 0 us
  local copies, waits for them, and re-layouts: 3.63 us -> 7.74 us
    pallas_call x0 -> x1, Pallas kernels: none -> 78.6 us  [one_kernel(): pl.pallas_call(functools.partial(step_kernel, tps, reps), out_shape=[jax....]
    psum x2 -> x0, blocking collectives: 56.1 us -> none  [the longest x1 39.7 us: per_device(): lax.psum((jnp.sum(jnp.exp(capped), 1), picked_part), ('tp', 'rep'))]
    psum x1 -> x0, waiting for transfers between devices: 44.5 us -> none  [per_device(): heads = lax.psum(partial_value, 'tp')]
    dot_general x5 -> x0, matrix products: 35.8 us -> none  [the longest x1 30.2 us: per_device(): lax.dot_general(normed, embedding, contract, preferred_element_type=jnp.f...]
    all_gather x1 -> x0, blocking collectives: 15.9 us -> none  [per_device(): lax.all_gather(context, 'rep', axis=0, tiled=True)]
    all_gather x1 -> x0, waiting for transfers between devices: 14.5 us -> none  [per_device(): full = lax.all_gather(stream, 'rep', axis=1, tiled=True)]
    unnamed x20 -> x4, local copies, waits for them, and re-layouts: 0.05 us -> 6.39 us
    reduce_sum x3 -> x0, other arithmetic: 2.7 us -> none  [the longest x1 2.44 us: per_device(): scale = lax.rsqrt(jnp.mean(full * full, axis=1, keepdims=True) + 1e-06)]
  transfers between devices with their start and end apart: 2 -> 0, of which waited for: 2 -> 0; matrix products, arithmetic and copies ran while one was open for 0% -> 0% of each run, Pallas kernels for 0% -> 0%
where the time goes in v1:
time: 87.3 us; the launch traced here: 87 us
  Pallas kernels  78.6 us (90%)
  local copies, waits for them, and re-layouts  7.74 us (9%)
    pallas_call x1, Pallas kernels, one_kernel(): pl.pallas_call(functools.partial(step_kernel, tps, reps), out_shape=[jax....  78.6 us
    unnamed x4, local copies, waits for them, and re-layouts  6.39 us

profile of v1, /device:TPU:0, one launch (start us, length us, event | category | flops | bytes accessed | tf_op | source)
XLA Modules:
  0.0 87.0 jit_solution(563748527742019135)
XLA Ops:
  0.6 1.3 %reshape.25.gain = f32[1,4608]{1,0:T(1,128)} reshape(f32[4608]{0:T(1024)} %param.22) | data formatting | bytes 36864 | tf_op jit(solution)/shard_map/reshape | solution.py:522
  2.0 1.7 %copy.16.residual = bf16[128,576]{1,0:T(8,128)(2,1)} copy(bf16[128,576]{0,1:T(8,128)(2,1)} %param.21) | data formatting | bytes 294912 | tf_op args[7]
  3.7 2.4 %copy.17.proj_hbm = bf16[1024,576]{1,0:T(8,128)(2,1)} copy(bf16[1024,576]{0,1:T(8,128)(2,1)} %param.20) | data formatting | bytes 2359296 | tf_op args[6]
  6.1 78.6 %decode_step.1 = (f32[1,16]{1,0:T(1,128)}, f32[1,16]{1,0:T(1,128)}) custom-call(s32[16]{0:T(128)} %lengths.1, bf16[16,1024]{1,0:T(8,128)(2,1)} %queries.1, bf16[16,512]{1,0:T(8,128)(2,1)} %new_keys.1, bf16[16,512]{1,0:T(8,128)(2,1)} %new_values.1, bf16[128,576]{1,0:T(8,128)(2,1)} %copy.16.residual, f32[1,4608]{1,0:T(1,128)} %reshape.25.gain, ...), custom_call_target="tpu_custom_call" | custom-call | tf_op jit(solution)/shard_map/decode_step/pallas_call | solution.py:480
  84.8 1.1 %copy.20 = f32[16]{0:T(128)} copy(f32[16]{0:T(128)} %bitcast.11) | data formatting | bytes 128
  85.9 1.1 %copy.21 = f32[16]{0:T(128)} copy(f32[16]{0:T(128)} %bitcast.10) | data formatting | bytes 128

commit v2 on v1

--- a/solution.py
+++ b/solution.py
@@ -117,6 +117,20 @@
 def step_kernel(
     tps,
     reps,
+    lengths_hbm,
+    queries_hbm,
+    new_keys_hbm,
+    new_values_hbm,
+    residual_hbm,
+    gain_hbm,
+    targets_hbm,
+    rewards_hbm,
+    group_ids_hbm,
+    keys_hbm,
+    values_hbm,
+    proj_hbm,
+    table_hbm,
+    out,
     lengths,
     queries,
     new_keys,
@@ -124,19 +138,15 @@
     residual,
     gain,
     targets,
-    old_sums,
     rewards,
     group_ids,
-    keys_hbm,
-    values_hbm,
-    proj_hbm,
-    table_hbm,
-    logprob_out,
-    advantage_out,
     keys,
     values,
     proj,
     table,
+    raw,
+    total_acc,
+    picked_acc,
     q_rows,
     nk_rows,
     nv_rows,
@@ -144,6 +154,7 @@
     context,
     partial,
     reduced,
+    resid,
     blocks,
     normed,
     reward_rows,
@@ -165,7 +176,7 @@
     heads = queries.shape[1] // depth
     ratio = heads // heads_kv
     total_samp = samp * reps
-    cols = residual.shape[1]
+    cols = residual.shape[0]
     padded = blocks.shape[2]
     share = total_samp // tps
     vocab_rows, width = table_hbm.shape
@@ -191,13 +202,25 @@
             table_sem.at[slot],
         )
 
-    key_copies = [pltpu.make_async_copy(keys_hbm, keys, local_sem.at[0])]
-    value_copies = [pltpu.make_async_copy(values_hbm, values, local_sem.at[1])]
-    proj_copy = pltpu.make_async_copy(proj_hbm, proj, local_sem.at[2])
-    for copy in key_copies + value_copies + [proj_copy]:
+    moves = [
+        (rewards_hbm, rewards),
+        (group_ids_hbm, group_ids),
+        (queries_hbm, queries),
+        (new_keys_hbm, new_keys),
+        (new_values_hbm, new_values),
+        (lengths_hbm, lengths),
+        (keys_hbm, keys),
+        (values_hbm, values),
+        (proj_hbm, proj),
+        (residual_hbm, residual),
+        (gain_hbm, gain),
+        (targets_hbm, targets),
+    ]
+    copies = [
+        pltpu.make_async_copy(src, dst, local_sem.at[n]) for n, (src, dst) in enumerate(moves)
+    ]
+    for copy in copies:
         copy.start()
-    for index in range(SLOTS):
-        table_copy(index, index).start()
 
     barrier = pltpu.get_barrier_semaphore()
     for k in range(1, tps):
@@ -231,6 +254,8 @@
             device_id_type=MESH,
         ).wait_recv()
 
+    for copy in copies[0:6]:
+        copy.wait()
     reward_rows[r] = jnp.zeros(reward_rows.shape[1:], jnp.float32)
     reward_rows[r, 0:1, 0:samp] = rewards[...]
     reward_rows[r, 1:2, 0:samp] = group_ids[...].astype(jnp.float32)
@@ -243,8 +268,9 @@
 
     head_group = lax.broadcasted_iota(jnp.int32, (heads, span), 0) // ratio
     position = lax.broadcasted_iota(jnp.int32, (heads, span), 1)
-    for copy in key_copies:
-        copy.wait()
+    copies[6].wait()
+    for index in range(SLOTS):
+        table_copy(index, index).start()
     probs = []
     own_probs = []
     for s in range(samp):
@@ -265,8 +291,7 @@
         total = jnp.sum(expo, 1, keepdims=True) + own_exp
         probs.append((expo / total).astype(jnp.bfloat16).astype(jnp.float32))
         own_probs.append((own_exp / total).astype(jnp.bfloat16).astype(jnp.float32))
-    for copy in value_copies:
-        copy.wait()
+    copies[7].wait()
     for s in range(samp):
         spread = jnp.concatenate(
             [jnp.where(head_group == g, probs[s], 0.0) for g in range(heads_kv)], axis=1
@@ -299,18 +324,25 @@
         q = lax.rem(partner + 2 * k, reps)
         received(ctx_slot(q), ctx_sem.at[q])
 
-    proj_copy.wait()
-    product = jnp.dot(context[...], proj[...], preferred_element_type=jnp.float32)
+    for copy in copies[8:]:
+        copy.wait()
+    product = lax.dot_general(
+        context[...], proj[...], (((1,), (1,)), ((), ())), preferred_element_type=jnp.float32
+    )
     for k in range(tps):
         partial[k] = product[k * share : (k + 1) * share]
     for k in range(1, tps):
         u = lax.rem(t + k, tps)
         send(partial.at[u], reduced.at[t], red_sem.at[t], (u, r))
     reduced[t] = partial[t]
-    own_gain = gain[:, 0:cols]
+    gain_row = jnp.concatenate([gain[n : n + 1] for n in range(gain.shape[0])], axis=1)
+    own_gain = gain_row[:, 0:cols]
     for q in range(1, reps):
-        own_gain = jnp.where(r == q, gain[:, q * cols : (q + 1) * cols], own_gain)
-    rest = residual[pl.ds(pl.multiple_of(t * share, share), share)].astype(jnp.float32)
+        own_gain = jnp.where(r == q, gain_row[:, q * cols : (q + 1) * cols], own_gain)
+    turned = jnp.transpose(residual[...].astype(jnp.float32))
+    for k in range(tps):
+        resid[k] = turned[k * share : (k + 1) * share]
+    rest = resid[t]
     for k in range(1, tps):
         u = lax.rem(t + k, tps)
         received(reduced.at[u], red_sem.at[u])
@@ -363,26 +395,24 @@
         normed[:, 2 * z * cols : 2 * (z + 1) * cols] = pair.astype(jnp.bfloat16)
         squares = squares + jnp.sum(left[:, cols:padded], 1, keepdims=True)
         squares = squares + jnp.sum(right[:, cols:padded], 1, keepdims=True)
-    scale = lax.rsqrt(squares / width + 1e-06)
+    scale = lax.rsqrt(squares / width + 1e-06) / 30.0
     wanted = as_column(targets[...].astype(jnp.float32), total_samp).astype(jnp.int32)
     wanted = wanted - (t * reps + r) * vocab_rows
 
-    def score(rows, first, carry):
-        total, picked = carry
-        logits = lax.dot_general(
+    def product_of(rows, half):
+        raw[half, :, 0 : rows.shape[0]] = lax.dot_general(
             normed[...], rows, (((1,), (1,)), ((), ())), preferred_element_type=jnp.float32
         )
-        capped = 30.0 * jnp.tanh(logits * scale / 30.0)
-        entry = lax.broadcasted_iota(jnp.int32, capped.shape, 1) + first
-        total = total + jnp.sum(jnp.exp(capped), 1, keepdims=True)
-        picked = picked + jnp.sum(jnp.where(entry == wanted, capped, 0.0), 1, keepdims=True)
-        return total, picked
-
-    def visit(index, carry):
-        slot = lax.rem(index, SLOTS)
-        table_copy(index, slot).wait()
-        carry = score(table[slot], index * ROWS_PER_BLOCK, carry)
-
+
+    def score(half, count, first):
+        for low in range(0, count, 128):
+            lanes = min(128, count - low)
+            capped = 30.0 * jnp.tanh(raw[half, :, low : low + lanes] * scale)
+            entry = lax.broadcasted_iota(jnp.int32, capped.shape, 1) + (first + low)
+            total_acc[:, 0:lanes] += jnp.exp(capped)
+            picked_acc[:, 0:lanes] += jnp.where(entry == wanted, capped, 0.0)
+
+    def refill(index, slot):
         @pl.when(index + SLOTS < full)
         def _():
             table_copy(index + SLOTS, slot).start()
@@ -393,13 +423,33 @@
             def _():
                 tail_copy().start()
 
-        return carry
-
-    zero = jnp.zeros((total_samp, 1), jnp.float32)
-    carry = lax.fori_loop(0, full, visit, (zero, zero))
+    total_acc[...] = jnp.zeros_like(total_acc)
+    picked_acc[...] = jnp.zeros_like(picked_acc)
+    table_copy(0, 0).wait()
+    product_of(table[0], 0)
+    refill(0, 0)
+
+    def visit(pair, nothing):
+        for half in (1, 0):
+            index = 2 * pair + (1 if half else 2)
+            slot = lax.rem(index, SLOTS)
+            table_copy(index, slot).wait()
+            product_of(table[slot], half)
+            score(1 - half, ROWS_PER_BLOCK, (index - 1) * ROWS_PER_BLOCK)
+            refill(index, slot)
+        return nothing
+
+    lax.fori_loop(0, (full - 1) // 2, visit, 0)
     if tail:
         tail_copy().wait()
-        carry = score(table[full % SLOTS, 0:tail], full * ROWS_PER_BLOCK, carry)
+        product_of(table[full % SLOTS, 0:tail], 1)
+    score(0, ROWS_PER_BLOCK, (full - 1) * ROWS_PER_BLOCK)
+    if tail:
+        score(1, tail, full * ROWS_PER_BLOCK)
+    carry = (
+        jnp.sum(total_acc[...], 1, keepdims=True),
+        jnp.sum(picked_acc[...], 1, keepdims=True),
+    )
 
     final_tp[t] = jnp.zeros(final_tp.shape[1:], jnp.float32)
     final_tp[t, 0:1] = as_row(carry[0], total_samp)
@@ -417,8 +467,7 @@
         group_sum = group_sum + jnp.sum(
             jnp.where(same, reward_rows[q, 0:1, 0:samp], 0.0), 1, keepdims=True
         )
-    group_sum = as_row(group_sum, samp)
-    advantage_out[...] = rewards[...] - (group_sum - rewards[...]) / (GROUP - 1.0)
+    out[1:2] = as_row(group_sum, samp)
 
     for k in range(1, tps):
         u = lax.rem(t + k, tps)
@@ -440,7 +489,7 @@
         lax.broadcasted_iota(jnp.int32, (samp, total_samp), 0) + r * samp
     )
     own_rows = jnp.sum(jnp.where(chosen, logprob, 0.0), 1, keepdims=True)
-    logprob_out[...] = old_sums[...] + as_row(own_rows, samp)
+    out[0:1] = as_row(own_rows, samp)
     for copy in sent:
         copy.wait_send()
 
@@ -474,19 +523,31 @@
         + (tps - 1) + (reps - 1)
     )
     vmem = pl.BlockSpec(memory_space=pltpu.VMEM)
-    smem = pl.BlockSpec(memory_space=pltpu.SMEM)
     hbm = pl.BlockSpec(memory_space=pltpu.HBM)
     dma = pltpu.SemaphoreType.DMA
-    logprob, advantage = pl.pallas_call(
+    lanes_gain = norm_gain.reshape(-1, 128)
+    sums = pl.pallas_call(
         functools.partial(step_kernel, tps, reps),
-        out_shape=[jax.ShapeDtypeStruct((1, samp), jnp.float32)] * 2,
-        in_specs=[smem] + [vmem] * 9 + [hbm] * 4,
-        out_specs=[vmem, vmem],
+        out_shape=jax.ShapeDtypeStruct((2, samp), jnp.float32),
+        in_specs=[hbm] * 13,
+        out_specs=vmem,
         scratch_shapes=[
+            pltpu.SMEM((samp,), jnp.int32),
+            pltpu.VMEM(queries.shape, queries.dtype),
+            pltpu.VMEM(new_keys.shape, new_keys.dtype),
+            pltpu.VMEM(new_values.shape, new_values.dtype),
+            pltpu.VMEM(residual.shape[::-1], residual.dtype),
+            pltpu.VMEM(lanes_gain.shape, jnp.float32),
+            pltpu.VMEM((1, total_samp), jnp.int32),
+            pltpu.VMEM((1, samp), jnp.float32),
+            pltpu.VMEM((1, samp), jnp.int32),
             pltpu.VMEM(stored_keys.shape, stored_keys.dtype),
             pltpu.VMEM(stored_values.shape, stored_values.dtype),
-            pltpu.VMEM(out_proj.shape, out_proj.dtype),
+            pltpu.VMEM(out_proj.shape[::-1], out_proj.dtype),
             pltpu.VMEM((SLOTS, ROWS_PER_BLOCK, embedding.shape[1]), embedding.dtype),
+            pltpu.VMEM((2, total_samp, ROWS_PER_BLOCK), jnp.float32),
+            pltpu.VMEM((total_samp, 128), jnp.float32),
+            pltpu.VMEM((total_samp, 128), jnp.float32),
             pltpu.VMEM((samp, heads, depth), jnp.float32),
             pltpu.VMEM((samp, heads, depth), jnp.float32),
             pltpu.VMEM((samp, heads, depth), jnp.float32),
@@ -494,12 +555,13 @@
             pltpu.VMEM((total_samp, heads * depth), jnp.bfloat16),
             pltpu.VMEM((tps, share, cols), jnp.float32),
             pltpu.VMEM((tps, share, cols), jnp.float32),
+            pltpu.VMEM((tps, share, cols), jnp.float32),
             pltpu.VMEM((reps, total_samp, padded), jnp.bfloat16),
             pltpu.VMEM((total_samp, embedding.shape[1]), jnp.bfloat16),
             pltpu.VMEM((reps, 8, 128), jnp.float32),
             pltpu.VMEM((tps, 8, total_samp), jnp.float32),
             pltpu.VMEM((reps, 8, total_samp), jnp.float32),
-            dma((3,)),
+            dma((12,)),
             dma((SLOTS,)),
             dma((sends,)),
             dma((reps,)),
@@ -518,18 +580,17 @@
         queries,
         new_keys,
         new_values,
-        residual,
-        norm_gain.reshape(1, -1),
+        residual.T,
+        lanes_gain,
         targets.reshape(1, -1),
-        old_sums.reshape(1, -1),
         rewards.reshape(1, -1),
         group_ids.reshape(1, -1),
         stored_keys,
         stored_values,
-        out_proj,
+        out_proj.T,
         embedding,
     )
-    return logprob.reshape(-1), advantage.reshape(-1)
+    return old_sums + sums[0], rewards - (sums[1] - rewards) / (GROUP - 1.0)
 
 
 def fits_one_kernel(tps, reps, stored_keys, out_proj, residual, embedding):
@@ -544,8 +605,10 @@
         and total_samp == 128
         and total_samp % (16 * tps) == 0
         and 2 * out_proj.shape[1] % 128 == 0
+        and out_proj.shape[1] % 16 == 0
         and embedding.shape[0] >= SLOTS * ROWS_PER_BLOCK
         and embedding.shape[0] % 16 == 0
+        and embedding.shape[0] // ROWS_PER_BLOCK % 2 == 1
         and embedding.shape[1] == reps * out_proj.shape[1]
     )
 

time: 87.3 us -> 68.7 us (0.79)
  Pallas kernels: 78.6 us -> 66.6 us
  local copies, waits for them, and re-layouts: 7.74 us -> 0.01 us
  other arithmetic: 0 us -> 1.26 us
    pallas_call x1, Pallas kernels: 78.6 us -> 66.6 us  [one_kernel(): pl.pallas_call(functools.partial(step_kernel, tps, reps), out_shape=jax.S...]
    unnamed x4, local copies, waits for them, and re-layouts: 6.39 us -> 0.01 us
    reshape x1 -> x0, local copies, waits for them, and re-layouts: 1.35 us -> none  [one_kernel(): norm_gain.reshape(1, -1)]
    sub x0 -> x1, other arithmetic: none -> 1.26 us  [one_kernel(): return (old_sums + sums[0], rewards - (sums[1] - rewards) / (GROUP - 1.0))]
where the time goes in v2:
time: 68.7 us; the launch traced here: 68.6 us
  Pallas kernels  66.6 us (97%)
  other arithmetic  1.26 us (2%)
    pallas_call x1, Pallas kernels, one_kernel(): pl.pallas_call(functools.partial(step_kernel, tps, reps), out_shape=jax.S...  66.6 us

profile of v2, /device:TPU:0, one launch (start us, length us, event | category | flops | bytes accessed | tf_op | source)
XLA Modules:
  0.0 68.6 jit_solution(18104850384668367156)
XLA Ops:
  0.6 0.0 copy-start
  0.6 0.0 copy-start.1
  0.7 66.6 %decode_step.1 = f32[2,16]{1,0:T(2,128)} custom-call(s32[16]{0:T(128)} %lengths_hbm.1, bf16[16,1024]{1,0:T(8,128)(2,1)} %queries_hbm.1, bf16[16,512]{1,0:T(8,128)(2,1)} %new_keys_hbm.1, bf16[16,512]{1,0:T(8,128)(2,1)} %new_values_hbm.1, bf16[576,128]{1,0:T(8,128)(2,1)} %bitcast.15, f32[36,128]{1,0:T(8,128)} %bitcast.16, s32[1,128]{1,0:T(1,128)} %bitcast.18, ...), custom_call_target="tpu_custom_call" | custom-call | tf_op jit(solution)/shard_map/decode_step/pallas_call | solution.py:529
  67.3 0.0 copy-done
  67.3 0.0 copy-done.1
  67.3 1.3 %fusion.1 = (f32[16]{0:T(128)}, f32[16]{0:T(128)}) fusion(f32[16]{0:T(128)S(1)} %copy-done, f32[2,16]{1,0:T(2,128)} %decode_step.1, f32[16]{0:T(128)S(1)} %copy-done.1), kind=kLoop, calls=%fused_computation.2 | loop fusion | flops 64 | bytes 384 | tf_op jit(solution)/shard_map/sub | solution.py:593
Async XLA Ops:
  0.6 66.7 %copy-start = (f32[16]{0:T(128)S(1)}, f32[16]{0:T(128)}, u32[]{:S(2)}) copy-start(f32[16]{0:T(128)} %param.26) | copy-start | bytes 196
  0.6 66.7 %copy-start.1 = (f32[16]{0:T(128)S(1)}, f32[16]{0:T(128)}, u32[]{:S(2)}) copy-start(f32[16]{0:T(128)} %param.25) | copy-start | bytes 196

commit v3 on v2

--- a/solution.py
+++ b/solution.py
@@ -330,26 +330,25 @@
         context[...], proj[...], (((1,), (1,)), ((), ())), preferred_element_type=jnp.float32
     )
     for k in range(tps):
-        partial[k] = product[k * share : (k + 1) * share]
+        partial[k] = product[k * share : (k + 1) * share].astype(jnp.bfloat16)
     for k in range(1, tps):
         u = lax.rem(t + k, tps)
         send(partial.at[u], reduced.at[t], red_sem.at[t], (u, r))
-    reduced[t] = partial[t]
     gain_row = jnp.concatenate([gain[n : n + 1] for n in range(gain.shape[0])], axis=1)
     own_gain = gain_row[:, 0:cols]
     for q in range(1, reps):
         own_gain = jnp.where(r == q, gain_row[:, q * cols : (q + 1) * cols], own_gain)
     turned = jnp.transpose(residual[...].astype(jnp.float32))
     for k in range(tps):
-        resid[k] = turned[k * share : (k + 1) * share]
+        rows = slice(k * share, (k + 1) * share)
+        resid[k] = turned[rows] + product[rows]
     rest = resid[t]
     for k in range(1, tps):
         u = lax.rem(t + k, tps)
         received(reduced.at[u], red_sem.at[u])
-    stream = reduced[0]
+    stream = rest
     for k in range(1, tps):
-        stream = stream + reduced[k]
-    stream = stream + rest
+        stream = stream + reduced[lax.rem(t + k, tps)].astype(jnp.float32)
     square = jnp.sum(stream * stream, 1, keepdims=True)
     high = square.astype(jnp.bfloat16).astype(jnp.float32)
     mid = (square - high).astype(jnp.bfloat16).astype(jnp.float32)
@@ -553,8 +552,8 @@
             pltpu.VMEM((samp, heads, depth), jnp.float32),
             pltpu.VMEM((samp, heads, depth), jnp.float32),
             pltpu.VMEM((total_samp, heads * depth), jnp.bfloat16),
-            pltpu.VMEM((tps, share, cols), jnp.float32),
-            pltpu.VMEM((tps, share, cols), jnp.float32),
+            pltpu.VMEM((tps, share, cols), jnp.bfloat16),
+            pltpu.VMEM((tps, share, cols), jnp.bfloat16),
             pltpu.VMEM((tps, share, cols), jnp.float32),
             pltpu.VMEM((reps, total_samp, padded), jnp.bfloat16),
             pltpu.VMEM((total_samp, embedding.shape[1]), jnp.bfloat16),

time: 68.7 us -> 67.7 us (0.985)
  Pallas kernels: 66.6 us -> 65.6 us
    pallas_call x1, Pallas kernels: 66.6 us -> 65.6 us  [one_kernel(): pl.pallas_call(functools.partial(step_kernel, tps, reps), out_shape=jax.S...]
where the time goes in v3:
time: 67.7 us; the launch traced here: 67.5 us
  Pallas kernels  65.6 us (97%)
  other arithmetic  1.26 us (2%)
  between operations  0.68 us (1%)
    pallas_call x1, Pallas kernels, one_kernel(): pl.pallas_call(functools.partial(step_kernel, tps, reps), out_shape=jax.S...  65.6 us

profile of v3, /device:TPU:0, one launch (start us, length us, event | category | flops | bytes accessed | tf_op | source)
XLA Modules:
  0.0 67.5 jit_solution(9459684687384674659)
XLA Ops:
  0.6 0.0 copy-start
  0.6 0.0 copy-start.1
  0.7 65.6 %decode_step.1 = f32[2,16]{1,0:T(2,128)} custom-call(s32[16]{0:T(128)} %lengths_hbm.1, bf16[16,1024]{1,0:T(8,128)(2,1)} %queries_hbm.1, bf16[16,512]{1,0:T(8,128)(2,1)} %new_keys_hbm.1, bf16[16,512]{1,0:T(8,128)(2,1)} %new_values_hbm.1, bf16[576,128]{1,0:T(8,128)(2,1)} %bitcast.15, f32[36,128]{1,0:T(8,128)} %bitcast.16, s32[1,128]{1,0:T(1,128)} %bitcast.18, ...), custom_call_target="tpu_custom_call" | custom-call | tf_op jit(solution)/shard_map/decode_step/pallas_call | solution.py:528
  66.2 0.0 copy-done
  66.2 0.0 copy-done.1
  66.2 1.3 %fusion.1 = (f32[16]{0:T(128)}, f32[16]{0:T(128)}) fusion(f32[16]{0:T(128)S(1)} %copy-done, f32[2,16]{1,0:T(2,128)} %decode_step.1, f32[16]{0:T(128)S(1)} %copy-done.1), kind=kLoop, calls=%fused_computation.2 | loop fusion | flops 64 | bytes 384 | tf_op jit(solution)/shard_map/sub | solution.py:592
Async XLA Ops:
  0.6 65.6 %copy-start = (f32[16]{0:T(128)S(1)}, f32[16]{0:T(128)}, u32[]{:S(2)}) copy-start(f32[16]{0:T(128)} %param.26) | copy-start | bytes 196
  0.6 65.6 %copy-start.1 = (f32[16]{0:T(128)S(1)}, f32[16]{0:T(128)}, u32[]{:S(2)}) copy-start(f32[16]{0:T(128)} %param.25) | copy-start | bytes 196
